TPU v7x, 32 devices: a whole 2x2x4 slice. The times are simulated.
32 devices in a mesh: dp: 8 (over z, x), latent: 4 (over y, core).
Axes of the slice: x: 2, y: 2, z: 4, core: 2. Of those that a mesh axis runs over, the one named last changes fastest.
Arguments:
- tokens: bfloat16 [1024, 1536], P('dp'), may hold values from -6 to 6
- enc_weight: bfloat16 [1536, 32768], P(None, ('dp', 'latent')), may hold values from -0.15625 to 0.15625
- enc_bias: float32 [32768], P(('dp', 'latent')), may hold values from -3 to 3
- dec_weight: bfloat16 [32768, 1536], P(('dp', 'latent')), may hold values from -0.0625 to 0.0625
- dec_bias: float32 [1536], replicated, may hold values from -3 to 3
- slot_token: int32 [1024], P(('dp', 'latent')), may hold values from 0 to 7
- slot_latent: int32 [1024], P(('dp', 'latent')), may hold values from 0 to 7
- slot_count: int32 [32], P(('dp', 'latent')), may hold values from 6 to 32, as said below
Outputs:
- enc_grad: bfloat16 [1536, 32768], P(None, ('dp', 'latent'))
- dec_grad: bfloat16 [32768, 1536], P(('dp', 'latent'))
- enc_bias_grad: float32 [32768], P(('dp', 'latent'))
- dec_bias_grad: float32 [1536], replicated
- mean_error: float32 [], replicated
Inputs may be any that keep to these rules, and one draw needn't show every extreme that they name: `slot_count`: slot lists of one device never repeat a (token block, latent block) pair among its 32 slots; entries past a device's count name valid blocks and are ignored; some device has all 32 slots live in every draw.
All inputs are finite; a program needn't handle non-finite values.
Results may differ from a plain program's by a relative error of at most 0.0065.
Values may be sent and summed in bfloat16 or wider, within the bound.
A program may use at most 128 MiB of HBM per device.

v0:
```python
import jax
import jax.numpy as jnp
from jax import lax
from jax.sharding import PartitionSpec as P

BLK = 128


def local(tokens, enc_weight, enc_bias, dec_weight, dec_bias, slot_token, slot_latent, slot_count):
    block_size = BLK
    gathered = lax.all_gather(tokens, "dp", axis=0, tiled=True)
    total_rows = gathered.shape[0]
    features = tokens.shape[1]
    capacity = slot_token.shape[0]
    live_count = slot_count[0]

    def forward_slot(slot_index, carried):
        activations, partial_value = carried
        row_start = slot_token[slot_index] * block_size
        col_start = slot_latent[slot_index] * block_size
        tok_rows = lax.dynamic_slice_in_dim(gathered, row_start, block_size, 0)
        enc_block = lax.dynamic_slice_in_dim(enc_weight, col_start, block_size, 1)
        bias_block = lax.dynamic_slice_in_dim(enc_bias, col_start, block_size, 0)
        active = (
            jnp.dot(tok_rows, enc_block, preferred_element_type=jnp.float32) + bias_block[None, :]
        ).astype(jnp.bfloat16)
        dec_block = lax.dynamic_slice_in_dim(dec_weight, col_start, block_size, 0)
        contrib = jnp.dot(active, dec_block, preferred_element_type=jnp.float32)
        previous = lax.dynamic_slice_in_dim(partial_value, row_start, block_size, 0)
        partial_value = lax.dynamic_update_slice_in_dim(
            partial_value, previous + contrib, row_start, 0
        )
        activations = lax.dynamic_update_index_in_dim(activations, active, slot_index, 0)
        return (activations, partial_value)

    empty_acts = jnp.zeros((capacity, block_size, block_size), jnp.bfloat16)
    empty_sum = jnp.zeros((total_rows, features), jnp.float32)
    activations, partial_value = lax.fori_loop(0, live_count, forward_slot, (empty_acts, empty_sum))
    share = lax.psum_scatter(partial_value, ("dp", "latent"), scatter_dimension=0, tiled=True)
    share_rows = share.shape[0]
    offset = lax.axis_index("latent") * share_rows
    token_share = lax.dynamic_slice_in_dim(tokens, offset, share_rows, 0)
    residual = share + dec_bias[None, :] - token_share.astype(jnp.float32)
    scaled = residual * 0.25
    squared, dec_bias_grad = lax.psum(
        (jnp.sum(residual * residual), jnp.sum(scaled, axis=0)), ("dp", "latent")
    )
    grad_all = lax.all_gather(scaled.astype(jnp.bfloat16), ("dp", "latent"), axis=0, tiled=True)
    mean_error = squared / (total_rows * features)

    def backward_slot(slot_index, gradients):
        enc_acc, dec_acc, bias_acc = gradients
        row_start = slot_token[slot_index] * block_size
        col_start = slot_latent[slot_index] * block_size
        tok_rows = lax.dynamic_slice_in_dim(gathered, row_start, block_size, 0)
        grad_block = lax.dynamic_slice_in_dim(grad_all, row_start, block_size, 0)
        dec_block = lax.dynamic_slice_in_dim(dec_weight, col_start, block_size, 0)
        pre_grad = lax.dot_general(
            grad_block, dec_block, (((1,), (1,)), ((), ())), preferred_element_type=jnp.float32
        )
        old_bias = lax.dynamic_slice_in_dim(bias_acc, col_start, block_size, 0)
        bias_acc = lax.dynamic_update_slice_in_dim(
            bias_acc, old_bias + jnp.sum(pre_grad, axis=0), col_start, 0
        )
        pre_half = pre_grad.astype(jnp.bfloat16)
        enc_term = lax.dot_general(
            tok_rows, pre_half, (((0,), (0,)), ((), ())), preferred_element_type=jnp.float32
        )
        old_enc = lax.dynamic_slice_in_dim(enc_acc, col_start, block_size, 1)
        enc_acc = lax.dynamic_update_slice_in_dim(enc_acc, old_enc + enc_term, col_start, 1)
        dec_term = lax.dot_general(
            activations[slot_index],
            grad_block,
            (((0,), (0,)), ((), ())),
            preferred_element_type=jnp.float32,
        )
        old_dec = lax.dynamic_slice_in_dim(dec_acc, col_start, block_size, 0)
        dec_acc = lax.dynamic_update_slice_in_dim(dec_acc, old_dec + dec_term, col_start, 0)
        return (enc_acc, dec_acc, bias_acc)

    latents_here = enc_weight.shape[1]
    start_grads = (
        jnp.zeros((features, latents_here), jnp.float32),
        jnp.zeros((latents_here, features), jnp.float32),
        jnp.zeros((latents_here,), jnp.float32),
    )
    enc_acc, dec_acc, bias_acc = lax.fori_loop(0, live_count, backward_slot, start_grads)
    return (
        enc_acc.astype(jnp.bfloat16),
        dec_acc.astype(jnp.bfloat16),
        bias_acc,
        dec_bias_grad,
        mean_error,
    )


def solution(mesh):
    in_specs = (
        P("dp", None),
        P(None, ("dp", "latent")),
        P(("dp", "latent")),
        P(("dp", "latent"), None),
        P(),
        P(("dp", "latent")),
        P(("dp", "latent")),
        P(("dp", "latent")),
    )
    out_specs = (
        P(None, ("dp", "latent")),
        P(("dp", "latent"), None),
        P(("dp", "latent")),
        P(),
        P(),
    )
    return jax.shard_map(local, mesh=mesh, in_specs=in_specs, out_specs=out_specs, check_vma=False)
```

profile of v0, /device:TPU:7, one launch (start us, length us, event | category | flops | bytes accessed | tf_op | source)
XLA Modules:
  0.0 829.1 jit_solution(1080155368049432398)
XLA Ops:
  8.0 60.8 %all-gather.3.cloned.1.call-done = bf16[1024,1536]{1,0:T(8,128)(2,1)} async-done(((bf16[128,1536]{1,0:T(8,128)(2,1)}), bf16[1024,1536]{1,0:T(8,128)(2,1)}) %all-gather.3.cloned.1.call-update) | async-done | bytes 3145744 | tf_op jit(solution)/shard_map/all_gather | solution.py:11
  69.0 3.4 broadcast.5.clone
  72.4 247.6 %while.26 = (s32[]{:T(128)}, bf16[32,128,128]{2,1,0:T(8,128)(2,1)S(1)}, f32[1024,1536]{1,0:T(8,128)}, s32[]{:T(128)}, s32[32]{0:T(128)S(1)}, /*index=5*/bf16[102...) while((s32[]{:T(128)}, ...), condition=%wide.region_1.2_spmd, body=%wide.region_0.1_spmd.sunk | while | flops 100892688 | bytes 2852675 | solution.py:38
  320.1 114.0 %reduce-scatter.2.cloned.1.call-done = f32[32,1536]{1,0:T(8,128)} async-done(((f32[1024,1536]{1,0:T(8,128)}), f32[32,1536]{1,0:T(8,128)}) %reduce-scatter.2.cloned.1.call-update) | async-done | bytes 196624 | tf_op jit(solution)/shard_map/reduce_scatter | solution.py:39
  436.3 41.5 %all-reduce = (f32[1536]{0:T(1024)}, f32[]{:T(128)}) all-reduce(f32[1536]{0:T(1024)S(1)} %get-tuple-element.125, f32[]{:T(128)} %get-tuple-element.124), channel_id=1, replica_groups=mesh['dp'=8,'latent'=4] {'dp','latent'}, use_global_device_ids=true, to_apply=%region_7.8 | all-reduce | flops 1537 | bytes 12296 | tf_op jit(solution)/shard_map/psum | solution.py:45
  478.5 18.6 %all-gather.5.cloned.1.call-done = bf16[1024,1536]{1,0:T(8,128)(2,1)} async-done(((bf16[32,1536]{1,0:T(8,128)(2,1)}), bf16[1024,1536]{1,0:T(8,128)(2,1)}) %all-gather.5.cloned.1.call-update) | async-done | bytes 3145744 | tf_op jit(solution)/shard_map/all_gather | solution.py:48
  497.2 3.4 broadcast.5
  500.6 3.4 broadcast_in_dim.15
  504.0 310.2 %while.27 = (s32[]{:T(128)}, f32[1536,1024]{1,0:T(8,128)}, f32[1024,1536]{1,0:T(8,128)}, f32[1024]{0:T(1024)S(1)}, s32[]{:T(128)}, /*index=5*/s32[32]{0:T(128)S(...) while((s32[]{:T(128)}, f32[1536,1024]{1,0:T(8,128)}, ...), condition=%wide.region_5.6_spmd, body=%wide.region_3.0_spmd.sunk | while | flops 151420944 | bytes 4819283 | solution.py:87
  508.8 2.5 fusion.41
  511.3 2.5 fusion.42
  518.5 2.5 fusion.41
  528.2 2.5 fusion.41
  537.9 2.5 fusion.41
  547.5 2.5 fusion.41
  550.0 2.5 fusion.42
  557.3 2.5 fusion.41
  559.8 2.5 fusion.42
  567.0 2.5 fusion.41
  576.7 2.5 fusion.41
  586.4 2.5 fusion.41
  596.0 2.5 fusion.41
  605.7 2.5 fusion.41
  615.4 2.5 fusion.41
  617.8 2.5 fusion.42
  625.0 2.5 fusion.41
  634.7 2.5 fusion.41
  644.3 2.5 fusion.41
  654.0 2.5 fusion.41
  663.6 2.5 fusion.41
  673.3 2.5 fusion.41
  683.0 2.5 fusion.41
  692.6 2.5 fusion.41
  695.1 2.5 fusion.42
  702.4 2.5 fusion.41
  712.0 2.5 fusion.41
  721.7 2.5 fusion.41
  724.1 2.5 fusion.42
  731.4 2.5 fusion.41
  741.1 2.5 fusion.41
  750.7 2.5 fusion.41
  760.4 2.5 fusion.41
  770.1 2.5 fusion.41
  779.7 2.5 fusion.41
  789.4 2.5 fusion.41
  799.0 2.5 fusion.41
  808.7 2.5 fusion.41
  814.3 5.1 convert_element_type.20
  (334 shorter events, 340.4 us)
Async XLA Ops:
  7.2 65.2 %copy-start.3 = (s32[32]{0:T(128)S(1)}, s32[32]{0:T(128)}, u32[]{:S(2)}) copy-start(s32[32]{0:T(128)} %param.18) | copy-start | bytes 388
  7.2 65.2 %copy-start.4 = (s32[32]{0:T(128)S(1)}, s32[32]{0:T(128)}, u32[]{:S(2)}) copy-start(s32[32]{0:T(128)} %param.17) | copy-start | bytes 388
  7.2 61.5 %all-gather.3.cloned.1.call-start = ((), (), s32[]{:S(2)}) async-start(), calls=%async_computation.1 | async-start | bytes 3538944 | tf_op jit(solution)/shard_map/all_gather | solution.py:11
  7.9 426.1 %reduce-scatter.2.cloned.1.call-start = ((), (), s32[]{:S(2)}) async-start(), calls=%async_computation.2 | async-start | bytes 6488064 | tf_op jit(solution)/shard_map/reduce_scatter | solution.py:39
  320.0 114.1 %copy-start.2 = (f32[1536]{0:T(1024)S(1)}, f32[1536]{0:T(1024)}, u32[]{:S(2)}) copy-start(f32[1536]{0:T(1024)} %param.16) | copy-start | bytes 18436
  320.0 177.2 %all-gather.5.cloned.1.call-start = ((), (), s32[]{:S(2)}) async-start(), calls=%async_computation.3 | async-start | bytes 3244032 | tf_op jit(solution)/shard_map/all_gather | solution.py:48
  814.2 7.2 copy-start.1
  814.3 5.1 copy-start
Sparse Core Ops, SparseCore 0:
  10.2 58.5 all-gather.2
  320.1 113.8 reduce-scatter.1
  437.5 59.6 all-gather.4
where the time goes:
time: 836 us; the launch traced here: 829 us
  matrix products  324 us (39%)
  waiting for transfers between devices  194 us (23%)
  loops' own time  128 us (15%)
  local copies, waits for them, and re-layouts  110 us (13%)
  blocking collectives  41.5 us (5%)
  between operations  15.6 us (2%)
  other arithmetic  15.4 us (2%)
    reduce_scatter x1, waiting for transfers between devices, local(): lax.psum_scatter(partial_value, ('dp', 'latent'), scatter_dimension=0, ti...  114 us
    dot_general x32, matrix products, backward_slot(): lax.dot_general(tok_rows, pre_half, (((0,), (0,)), ((), ())), preferred_e...  79.5 us
    dot_general x32, matrix products, backward_slot(): lax.dot_general(activations[slot_index], grad_block, (((0,), (0,)), ((),...  78.3 us
    dot_general x32, matrix products, forward_slot(): contrib = jnp.dot(active, dec_block, preferred_element_type=jnp.float32)  77.1 us
    another operation x1, loops' own time, local(): lax.fori_loop(0, live_count, backward_slot, start_grads)  64.1 us
    another operation x1, loops' own time, local(): lax.fori_loop(0, live_count, forward_slot, (empty_acts, empty_sum))  64.1 us
    all_gather x1, waiting for transfers between devices, local(): gathered = lax.all_gather(tokens, 'dp', axis=0, tiled=True)  60.8 us
    dot_general x32, matrix products, backward_slot(): lax.dot_general(grad_block, dec_block, (((1,), (1,)), ((), ())), preferre...  44.6 us
  transfers between devices with their start and end apart: 3, of which 3 were waited for; matrix products, arithmetic and copies ran while one was open for 0% of the time, Pallas kernels for 0%

commit v1 on v0

--- a/solution.py
+++ b/solution.py
@@ -8,7 +8,12 @@
 
 def local(tokens, enc_weight, enc_bias, dec_weight, dec_bias, slot_token, slot_latent, slot_count):
     block_size = BLK
-    gathered = lax.all_gather(tokens, "dp", axis=0, tiled=True)
+    ring = [tokens]
+    for hop in range(7):
+        ring.append(lax.ppermute(ring[-1], "dp", [(dev, (dev + 1) % 8) for dev in range(8)]))
+    gathered = jnp.roll(
+        jnp.concatenate(ring[::-1], axis=0), (lax.axis_index("dp") + 1) * ring[0].shape[0], axis=0
+    )
     total_rows = gathered.shape[0]
     features = tokens.shape[1]
     capacity = slot_token.shape[0]

time: 836 us -> 863 us (1.032)
  matrix products: 324 us -> 336 us
    ppermute x0 -> x7, waiting for transfers between devices: none -> 66.2 us  [local(): lax.ppermute(ring[-1], 'dp', [(dev, (dev + 1) % 8) for dev in range(8)])]
    all_gather x1 -> x0, waiting for transfers between devices: 60.8 us -> none  [local(): gathered = lax.all_gather(tokens, 'dp', axis=0, tiled=True)]
    dot_general x32, matrix products: 44.2 us -> 59.7 us  [forward_slot(): jnp.dot(tok_rows, enc_block, preferred_element_type=jnp.float32)]
  transfers between devices with their start and end apart: 3 -> 9, of which waited for: 3 -> 9; matrix products, arithmetic and copies ran while one was open for 0% -> 0% of each run, Pallas kernels for 0% -> 0%
where the time goes in v1:
time: 863 us; the launch traced here: 855 us
  matrix products  336 us (39%)
  waiting for transfers between devices  200 us (23%)
  loops' own time  128 us (15%)
  local copies, waits for them, and re-layouts  113 us (13%)
  blocking collectives  41.5 us (5%)
  between operations  16 us (2%)
  other arithmetic  15.3 us (2%)
    reduce_scatter x1, waiting for transfers between devices, local(): lax.psum_scatter(partial_value, ('dp', 'latent'), scatter_dimension=0, ti...  115 us
    dot_general x32, matrix products, backward_slot(): lax.dot_general(activations[slot_index], grad_block, (((0,), (0,)), ((),...  78.9 us
    dot_general x32, matrix products, forward_slot(): contrib = jnp.dot(active, dec_block, preferred_element_type=jnp.float32)  76.9 us
    dot_general x32, matrix products, backward_slot(): lax.dot_general(tok_rows, pre_half, (((0,), (0,)), ((), ())), preferred_e...  76.2 us
    ppermute x7, waiting for transfers between devices, local(): lax.ppermute(ring[-1], 'dp', [(dev, (dev + 1) % 8) for dev in range(8)])  66.2 us
    another operation x1, loops' own time, local(): lax.fori_loop(0, live_count, backward_slot, start_grads)  64.1 us
    another operation x1, loops' own time, local(): lax.fori_loop(0, live_count, forward_slot, (empty_acts, empty_sum))  64.1 us
    dot_general x32, matrix products, forward_slot(): jnp.dot(tok_rows, enc_block, preferred_element_type=jnp.float32)  59.7 us
  transfers between devices with their start and end apart: 9, of which 9 were waited for; matrix products, arithmetic and copies ran while one was open for 0% of the time, Pallas kernels for 0%

profile of v1, /device:TPU:7, one launch (start us, length us, event | category | flops | bytes accessed | tf_op | source)
XLA Modules:
  0.0 854.9 jit_solution(1532430630030133414)
XLA Ops:
  8.5 8.9 %collective-permute-done = bf16[128,1536]{1,0:T(8,128)(2,1)S(1)} collective-permute-done((bf16[128,1536]{1,0:T(8,128)(2,1)}, bf16[128,1536]{1,0:T(8,128)(2,1)S(1)}, u32[]{:S(2)}, u32[]{:S(2)}) %collective-permute-start) | collective-permute-done | bytes 393248 | tf_op jit(solution)/shard_map/ppermute | solution.py:13
  19.7 9.0 %collective-permute-done.1 = bf16[128,1536]{1,0:T(8,128)(2,1)S(1)} collective-permute-done((bf16[128,1536]{1,0:T(8,128)(2,1)S(1)}, bf16[128,1536]{1,0:T(8,128)(2,1)S(1)}, u32[]{:S(2)}, u32[]{:S(2)}) %collective-permute-start.1) | collective-permute-done | bytes 393248 | tf_op jit(solution)/shard_map/ppermute | solution.py:13
  29.7 10.1 %collective-permute-done.2 = bf16[128,1536]{1,0:T(8,128)(2,1)S(1)} collective-permute-done((bf16[128,1536]{1,0:T(8,128)(2,1)S(1)}, bf16[128,1536]{1,0:T(8,128)(2,1)S(1)}, u32[]{:S(2)}, u32[]{:S(2)}) %collective-permute-start.2) | collective-permute-done | bytes 393248 | tf_op jit(solution)/shard_map/ppermute | solution.py:13
  39.8 10.2 %collective-permute-done.3 = bf16[128,1536]{1,0:T(8,128)(2,1)S(1)} collective-permute-done((bf16[128,1536]{1,0:T(8,128)(2,1)S(1)}, bf16[128,1536]{1,0:T(8,128)(2,1)S(1)}, u32[]{:S(2)}, u32[]{:S(2)}) %collective-permute-start.3) | collective-permute-done | bytes 393248 | tf_op jit(solution)/shard_map/ppermute | solution.py:13
  50.0 9.4 %collective-permute-done.4 = bf16[128,1536]{1,0:T(8,128)(2,1)S(1)} collective-permute-done((bf16[128,1536]{1,0:T(8,128)(2,1)S(1)}, bf16[128,1536]{1,0:T(8,128)(2,1)S(1)}, u32[]{:S(2)}, u32[]{:S(2)}) %collective-permute-start.4) | collective-permute-done | bytes 393248 | tf_op jit(solution)/shard_map/ppermute | solution.py:13
  59.3 9.0 %collective-permute-done.5 = bf16[128,1536]{1,0:T(8,128)(2,1)S(1)} collective-permute-done((bf16[128,1536]{1,0:T(8,128)(2,1)S(1)}, bf16[128,1536]{1,0:T(8,128)(2,1)S(1)}, u32[]{:S(2)}, u32[]{:S(2)}) %collective-permute-start.5) | collective-permute-done | bytes 393248 | tf_op jit(solution)/shard_map/ppermute | solution.py:13
  68.4 9.5 %collective-permute-done.6 = bf16[128,1536]{1,0:T(8,128)(2,1)S(1)} collective-permute-done((bf16[128,1536]{1,0:T(8,128)(2,1)S(1)}, bf16[128,1536]{1,0:T(8,128)(2,1)S(1)}, u32[]{:S(2)}, u32[]{:S(2)}) %collective-permute-start.6) | collective-permute-done | bytes 393248 | tf_op jit(solution)/shard_map/ppermute | solution.py:13
  80.9 3.4 broadcast.6.clone
  84.4 262.8 %while.26 = (s32[]{:T(128)}, bf16[32,128,128]{2,1,0:T(8,128)(2,1)}, f32[1024,1536]{1,0:T(8,128)}, s32[]{:T(128)}, s32[32]{0:T(128)S(1)}, /*index=5*/bf16[1024,15...) while((s32[]{:T(128)}, bf16[32,128,128]{2,1,0:T(8,128)(2,1)}, ...), condition=%wide.region_1.2_spmd, body=%wide.region_0.1_spmd.sunk | while | flops 100892688 | bytes 2852675 | solution.py:43
  347.2 115.1 %reduce-scatter.2.cloned.1.call-done = f32[32,1536]{1,0:T(8,128)} async-done(((f32[1024,1536]{1,0:T(8,128)}), f32[32,1536]{1,0:T(8,128)}) %reduce-scatter.2.cloned.1.call-update) | async-done | bytes 196624 | tf_op jit(solution)/shard_map/reduce_scatter | solution.py:44
  464.5 41.5 %all-reduce = (f32[1536]{0:T(1024)}, f32[]{:T(128)}) all-reduce(f32[1536]{0:T(1024)S(1)} %get-tuple-element.125, f32[]{:T(128)} %get-tuple-element.124), channel_id=1, replica_groups=mesh['dp'=8,'latent'=4] {'dp','latent'}, use_global_device_ids=true, to_apply=%region_7.8 | all-reduce | flops 1537 | bytes 12296 | tf_op jit(solution)/shard_map/psum | solution.py:50
  506.7 18.7 %all-gather.2.cloned.1.call-done = bf16[1024,1536]{1,0:T(8,128)(2,1)} async-done(((bf16[32,1536]{1,0:T(8,128)(2,1)}), bf16[1024,1536]{1,0:T(8,128)(2,1)}) %all-gather.2.cloned.1.call-update) | async-done | bytes 3145744 | tf_op jit(solution)/shard_map/all_gather | solution.py:53
  525.4 3.4 broadcast.6
  528.8 3.4 broadcast_in_dim.15
  532.3 307.5 %while.27 = (s32[]{:T(128)}, f32[1536,1024]{1,0:T(8,128)}, f32[1024,1536]{1,0:T(8,128)}, f32[1024]{0:T(1024)S(1)}, s32[]{:T(128)}, /*index=5*/s32[32]{0:T(128)S(...) while((s32[]{:T(128)}, f32[1536,1024]{1,0:T(8,128)}, ...), condition=%wide.region_5.6_spmd, body=%wide.region_3.5_spmd.sunk | while | flops 151420944 | bytes 4819283 | solution.py:92
  539.4 2.5 fusion.42
  549.0 2.5 fusion.42
  558.6 2.5 fusion.42
  568.2 2.4 fusion.42
  577.7 2.5 fusion.42
  587.3 2.5 fusion.42
  597.0 2.4 fusion.42
  606.5 2.5 fusion.42
  616.1 2.5 fusion.42
  625.7 2.5 fusion.42
  635.3 2.5 fusion.42
  644.9 2.5 fusion.42
  654.5 2.5 fusion.42
  664.1 2.4 fusion.42
  673.6 2.5 fusion.42
  683.2 2.4 fusion.42
  692.7 2.5 fusion.42
  702.3 2.5 fusion.42
  711.9 2.5 fusion.42
  721.5 2.5 fusion.42
  731.2 2.4 fusion.42
  740.8 2.5 fusion.42
  750.3 2.5 fusion.42
  760.0 2.5 fusion.42
  769.6 2.4 fusion.42
  779.2 2.5 fusion.42
  788.7 2.5 fusion.42
  798.3 2.5 fusion.42
  807.9 2.5 fusion.42
  817.5 2.4 fusion.42
  827.0 2.5 fusion.42
  836.6 2.5 fusion.42
  839.8 5.1 convert_element_type.20
  (368 shorter events, 374.9 us)
Async XLA Ops:
  7.2 72.3 %copy-start.1 = (bf16[128,1536]{1,0:T(8,128)(2,1)S(1)}, bf16[128,1536]{1,0:T(8,128)(2,1)}, u32[]{:S(2)}) copy-start(bf16[128,1536]{1,0:T(8,128)(2,1)} %param.12) | copy-start | bytes 1179652
  7.2 455.1 %reduce-scatter.2.cloned.1.call-start = ((), (), s32[]{:S(2)}) async-start(), calls=%async_computation.1 | async-start | bytes 6488064 | tf_op jit(solution)/shard_map/reduce_scatter | solution.py:44
  7.2 10.3 %collective-permute-start = (bf16[128,1536]{1,0:T(8,128)(2,1)}, bf16[128,1536]{1,0:T(8,128)(2,1)S(1)}, u32[]{:S(2)}, u32[]{:S(2)}) collective-permute-start(bf16[128,1536]{1,0:T(8,128)(2,1)} %param.12), channel_id=1, source_target_pairs={{0,4},{4,8},{8,12},{12,16},{16,20},{20,24},{24,28},{28,0},{1,5},{5... | collective-permute-start | bytes 1179656 | tf_op jit(solution)/shard_map/ppermute | solution.py:13
  17.5 11.2 %collective-permute-start.1 = (bf16[128,1536]{1,0:T(8,128)(2,1)S(1)}, bf16[128,1536]{1,0:T(8,128)(2,1)S(1)}, u32[]{:S(2)}, u32[]{:S(2)}) collective-permute-start(bf16[128,1536]{1,0:T(8,128)(2,1)S(1)} %collective-permute-done), channel_id=1, source_target_pairs={{0,4},{4,8},{8,12},{12,16},{16,20},{20,24},{24,28},{28,0},{1,5},{5... | collective-permute-start | bytes 1179656 | tf_op jit(solution)/shard_map/ppermute | solution.py:13
  28.7 11.1 %collective-permute-start.2 = (bf16[128,1536]{1,0:T(8,128)(2,1)S(1)}, bf16[128,1536]{1,0:T(8,128)(2,1)S(1)}, u32[]{:S(2)}, u32[]{:S(2)}) collective-permute-start(bf16[128,1536]{1,0:T(8,128)(2,1)S(1)} %collective-permute-done.1), channel_id=1, source_target_pairs={{0,4},{4,8},{8,12},{12,16},{16,20},{20,24},{24,28},{28,0},{1,5},{5... | collective-permute-start | bytes 1179656 | tf_op jit(solution)/shard_map/ppermute | solution.py:13
  39.8 10.2 %collective-permute-start.3 = (bf16[128,1536]{1,0:T(8,128)(2,1)S(1)}, bf16[128,1536]{1,0:T(8,128)(2,1)S(1)}, u32[]{:S(2)}, u32[]{:S(2)}) collective-permute-start(bf16[128,1536]{1,0:T(8,128)(2,1)S(1)} %collective-permute-done.2), channel_id=1, source_target_pairs={{0,4},{4,8},{8,12},{12,16},{16,20},{20,24},{24,28},{28,0},{1,5},{5... | collective-permute-start | bytes 1179656 | tf_op jit(solution)/shard_map/ppermute | solution.py:13
  50.0 9.4 %collective-permute-start.4 = (bf16[128,1536]{1,0:T(8,128)(2,1)S(1)}, bf16[128,1536]{1,0:T(8,128)(2,1)S(1)}, u32[]{:S(2)}, u32[]{:S(2)}) collective-permute-start(bf16[128,1536]{1,0:T(8,128)(2,1)S(1)} %collective-permute-done.3), channel_id=1, source_target_pairs={{0,4},{4,8},{8,12},{12,16},{16,20},{20,24},{24,28},{28,0},{1,5},{5... | collective-permute-start | bytes 1179656 | tf_op jit(solution)/shard_map/ppermute | solution.py:13
  59.3 9.0 %collective-permute-start.5 = (bf16[128,1536]{1,0:T(8,128)(2,1)S(1)}, bf16[128,1536]{1,0:T(8,128)(2,1)S(1)}, u32[]{:S(2)}, u32[]{:S(2)}) collective-permute-start(bf16[128,1536]{1,0:T(8,128)(2,1)S(1)} %collective-permute-done.4), channel_id=1, source_target_pairs={{0,4},{4,8},{8,12},{12,16},{16,20},{20,24},{24,28},{28,0},{1,5},{5... | collective-permute-start | bytes 1179656 | tf_op jit(solution)/shard_map/ppermute | solution.py:13
  68.3 9.5 %collective-permute-start.6 = (bf16[128,1536]{1,0:T(8,128)(2,1)S(1)}, bf16[128,1536]{1,0:T(8,128)(2,1)S(1)}, u32[]{:S(2)}, u32[]{:S(2)}) collective-permute-start(bf16[128,1536]{1,0:T(8,128)(2,1)S(1)} %collective-permute-done.5), channel_id=1, source_target_pairs={{0,4},{4,8},{8,12},{12,16},{16,20},{20,24},{24,28},{28,0},{1,5},{5... | collective-permute-start | bytes 1179656 | tf_op jit(solution)/shard_map/ppermute | solution.py:13
  79.5 4.9 copy-start.4
  79.5 4.9 copy-start.6
  347.1 115.2 %copy-start.3 = (f32[1536]{0:T(1024)S(1)}, f32[1536]{0:T(1024)}, u32[]{:S(2)}) copy-start(f32[1536]{0:T(1024)} %param.16) | copy-start | bytes 18436
  347.2 178.2 %all-gather.2.cloned.1.call-start = ((), (), s32[]{:S(2)}) async-start(), calls=%async_computation.2 | async-start | bytes 3244032 | tf_op jit(solution)/shard_map/all_gather | solution.py:53
  525.4 6.9 copy-start.5
  525.4 6.9 copy-start.7
  839.8 7.2 copy-start.2
  839.8 5.1 copy-start
Sparse Core Ops, SparseCore 0:
  347.3 114.9 reduce-scatter.1
  465.8 59.6 all-gather.1
